TPU v7x, 512 devices: a whole 4x4x16 slice. The times are simulated.
512 devices in a mesh: gx: 16 (over x, y_lo, core), gy: 32 (over y_hi, z).
Axes of the slice: x: 4, y: 4 (y_hi: 2, y_lo: 2; y = y_hi * 2 + y_lo), z: 16, core: 2. Of those that a mesh axis runs over, the one named last changes fastest.
Arguments:
- plate_motion: bfloat16 [32, 64, 128, 2, 128], P('gx', 'gy'), may hold values from -6 to 6
- adjoint_load: bfloat16 [32, 64, 128, 2, 128], P('gx', 'gy'), may hold values from -6 to 6
- excitation: bfloat16 [32, 64, 128, 2, 128], P('gx', 'gy'), may hold values from -6 to 6
- coupling: bfloat16 [32, 64, 5, 2, 128, 128], P('gx', 'gy'), may hold values from -0.25 to 0.25
- joints: int32 [32, 64, 4], P('gx', 'gy'), may hold values 0 or 1
- hydro: bfloat16 [2, 16384, 16384], P(None, 'gx', 'gy'), may hold values from -0.046875 to 0.046875
- panel_map: bfloat16 [16384, 2, 2, 128], P(('gx', 'gy')), may hold values from -0.25 to 0.25
Outputs:
- residual: float32 [32, 64, 128, 2, 128], P('gx', 'gy')
- multiplier: float32 [32, 64, 128, 2, 128], P('gx', 'gy')
- sensitivity: float32 [32, 64], P('gx', 'gy')
All inputs are finite; a program needn't handle non-finite values. No bound on the sum of `joints` on one device may be relied on, other than what follows from the above.
Results may differ from a plain program's by a relative error of at most 0.0031.
Values may be sent and summed in bfloat16 or wider, within the bound.
A program may use at most 64 MiB of HBM per device.

v0:
```python
import math
import jax
import jax.numpy as jnp
from jax import lax
from jax.sharding import PartitionSpec as P


def extended(x, sides, width):
    for axis, dim in sides:
        size, length = (lax.axis_size(axis), x.shape[dim])
        up = [(i, (i + 1) % size) for i in range(size - 1)]
        down = [(j, i) for i, j in up]
        last = lax.slice_in_dim(x, length - width, length, axis=dim)
        first = lax.slice_in_dim(x, 0, width, axis=dim)
        before = lax.ppermute(last, axis, up)
        after = lax.ppermute(first, axis, down)
        x = jnp.concatenate([before, x, after], axis=dim)
    return x


def complex_apply(form, coupling, vector):
    real_c = coupling[..., 0, :, :]
    imag_c = coupling[..., 1, :, :]
    real_v = vector[..., 0, :]
    imag_v = vector[..., 1, :]

    def mult(matrix, values):
        return jnp.einsum(form, matrix, values, preferred_element_type=jnp.float32)

    return jnp.stack(
        [mult(real_c, real_v) - mult(imag_c, imag_v), mult(real_c, imag_v) + mult(imag_c, real_v)],
        axis=-2,
    )


def adjoint_apply(form, coupling, vector):
    real_c = coupling[..., 0, :, :]
    imag_c = coupling[..., 1, :, :]
    real_v = vector[..., 0, :]
    imag_v = vector[..., 1, :]

    def mult(matrix, values):
        return jnp.einsum(form, matrix, values, preferred_element_type=jnp.float32)

    return jnp.stack(
        [mult(real_c, real_v) + mult(imag_c, imag_v), mult(real_c, imag_v) - mult(imag_c, real_v)],
        axis=-2,
    )


def plain_product(matrix, values):
    return jnp.dot(matrix, values, preferred_element_type=jnp.float32)


def flipped_product(matrix, values):
    return lax.dot_general(
        matrix, values, (((0,), (0,)), ((), ())), preferred_element_type=jnp.float32
    )


def on_device(plate_motion, adjoint_load, excitation, coupling, joints, hydro, panel_map):
    rows_count = plate_motion.shape[0]
    cols_count = plate_motion.shape[1]
    panel_count = panel_map.shape[0]
    unknowns = plate_motion.shape[4]
    cases = plate_motion.shape[2]
    links = joints.astype(jnp.float32)[:, :, :, None, None, None]
    padded = extended(plate_motion, (("gx", 0), ("gy", 1)), 1)
    beside_all = jnp.stack(
        [
            padded[0:rows_count, 1:-1],
            padded[2:, 1:-1],
            padded[1:-1, 0:cols_count],
            padded[1:-1, 2:],
        ],
        axis=2,
    )
    own = complex_apply("xyij,xyhj->xyhi", coupling[:, :, 0], plate_motion)
    structural = own + jnp.sum(
        links * complex_apply("xydij,xydhj->xydhi", coupling[:, :, 1:], beside_all), axis=2
    )
    outgoing = links * adjoint_apply("xydji,xyhj->xydhi", coupling[:, :, 1:], adjoint_load)
    own_adjoint = adjoint_apply("xyji,xyhj->xyhi", coupling[:, :, 0], adjoint_load)
    layered = extended(outgoing, (("gx", 0), ("gy", 1)), 1)
    incoming = (
        layered[2:, 1:-1, 0] + layered[:-2, 1:-1, 1] + layered[1:-1, 2:, 2] + layered[1:-1, :-2, 3]
    )
    lift = math.sqrt(rows_count * cols_count * unknowns / panel_count)
    motion_panels = jnp.einsum(
        "nxyk,xyhck->cnh", panel_map, plate_motion, preferred_element_type=jnp.float32
    ).astype(jnp.bfloat16)
    load_panels = jnp.einsum(
        "nxyk,xyhck->cnh", panel_map, adjoint_load, preferred_element_type=jnp.float32
    ).astype(jnp.bfloat16)
    piece = lax.all_gather(motion_panels, "gx", axis=1, tiled=True)
    first = plain_product(hydro[0], piece[0]) - plain_product(hydro[1], piece[1])
    second = plain_product(hydro[0], piece[1]) + plain_product(hydro[1], piece[0])
    pressure_part = jnp.stack([first, second])
    piece = lax.all_gather(load_panels, "gy", axis=1, tiled=True)
    first = flipped_product(hydro[0], piece[0]) + flipped_product(hydro[1], piece[1])
    second = flipped_product(hydro[0], piece[1]) - flipped_product(hydro[1], piece[0])
    reaction_part = jnp.stack([first, second])
    pressure_band = lax.psum(pressure_part, "gy")
    pressure = lax.dynamic_slice_in_dim(
        pressure_band, lax.axis_index("gy") * panel_count, panel_count, 1
    )
    reaction_band = lax.psum(reaction_part, "gx")
    reaction = lax.dynamic_slice_in_dim(
        reaction_band, lax.axis_index("gx") * panel_count, panel_count, 1
    )
    pressure = pressure.astype(jnp.bfloat16)
    reaction = reaction.astype(jnp.bfloat16)
    pressure_force = jnp.einsum(
        "nxyk,cnh->xyhck", panel_map, pressure, preferred_element_type=jnp.float32
    )
    reaction_force = jnp.einsum(
        "nxyk,cnh->xyhck", panel_map, reaction, preferred_element_type=jnp.float32
    )
    residual = structural + lift * pressure_force - excitation.astype(jnp.float32)
    multiplier = own_adjoint + incoming + lift * reaction_force
    sensitivity = jnp.sum(multiplier * own, axis=(2, 3, 4)) / math.sqrt(cases * unknowns)
    return (residual, multiplier, sensitivity)


def solution(mesh):
    placed = (
        P("gx", "gy", None, None, None),
        P("gx", "gy", None, None, None),
        P("gx", "gy", None, None, None),
        P("gx", "gy", None, None, None, None),
        P("gx", "gy", None),
        P(None, "gx", "gy"),
        P(("gx", "gy"), None, None, None),
    )
    return jax.shard_map(
        on_device,
        mesh=mesh,
        in_specs=placed,
        out_specs=(P("gx", "gy", None, None, None), P("gx", "gy", None, None, None), P("gx", "gy")),
        check_vma=False,
    )
```

profile of v0, /device:TPU:14, one launch (start us, length us, event | category | flops | bytes accessed | tf_op | source)
XLA Modules:
  0.0 440.0 jit_solution(6919222201309677431)
XLA Ops:
  2.4 1.9 collective-permute-start
  4.3 3.6 collective-permute-start.1
  8.0 1.3 slice_bitcast_fusion.2
  12.1 84.5 %all_gather.7 = bf16[2,1024,128]{2,1,0:T(8,128)(2,1)S(1)} all-gather(bf16[2,32,128]{2,1,0:T(8,128)(2,1)S(1)} %fusion.19), channel_id=1, replica_groups=mesh['gx'=16,'gy'=32] {'gy'}, dimensions={1}, use_global_device_ids=true | all-gather | bytes 540672 | tf_op jit(solution)/shard_map/all_gather | solution.py:99
  99.3 16.8 %all_gather.6 = bf16[2,512,128]{2,1,0:T(8,128)(2,1)S(1)} all-gather(bf16[2,32,128]{2,1,0:T(8,128)(2,1)S(1)} %fusion.20), channel_id=1, replica_groups=mesh['gx'=16,'gy'=32] {'gx'}, dimensions={1}, use_global_device_ids=true | all-gather | bytes 278528 | tf_op jit(solution)/shard_map/all_gather | solution.py:95
  118.9 2.0 fusion.15
  120.9 1.6 fusion.16
  126.1 1.3 collective-permute-start.2
  127.4 1.3 collective-permute-start.3
  130.8 2.9 collective-permute-done.2
  133.7 4.1 collective-permute-done.3
  140.1 1.3 maximum_multiply_fusion.1
  141.3 1.6 fusion.104
  142.9 1.9 collective-permute-start.4
  144.8 3.4 collective-permute-start.5
  150.7 18.0 %collective-permute-done.4 = f32[1,2,4,128,2,128]{5,3,1,0,4,2:T(8,128)} collective-permute-done((f32[1,2,4,128,2,128]{5,3,1,0,4,2:T(8,128)}, f32[1,2,4,128,2,128]{5,3,1,0,4,2:T(8,128)}, u32[]{:S(2)}, u32[]{:S(2)}) %collective-permute-start.4) | collective-permute-done | bytes 1048608 | tf_op jit(solution)/shard_map/ppermute | solution.py:16
  168.7 2.0 pad_maximum_fusion
  170.7 2.5 fusion.103
  173.2 1.4 collective-permute-start.6
  174.6 5.9 %collective-permute-start.7 = (f32[4,1,4,128,2,128]{5,3,1,0,4,2:T(8,128)}, f32[4,1,4,128,2,128]{5,3,1,0,4,2:T(8,128)}, u32[]{:S(2)}, u32[]{:S(2)}) collective-permute-start(f32[4,1,4,128,2,128]{5,3,1,0,4,2:T(8,128)} %get-tuple-element.10), channel_id=1, source_target_pairs={{0,1},{1,2},{2,3},{3,4},{4,5},{5,6},{6,7},{7,8},{8,9},{9,10},{10,1... | collective-permute-start | bytes 6291464 | tf_op jit(solution)/shard_map/ppermute | solution.py:15
  181.0 98.1 %all-reduce.2 = bf16[2,512,128]{2,1,0:T(8,128)(2,1)} all-reduce(f32[2,512,128]{2,1,0:T(8,128)} %pad_maximum_fusion.12), channel_id=1, replica_groups=mesh['gx'=16,'gy'=32] {'gx'}, use_global_device_ids=true, to_apply=%region_2.0 | all-reduce | flops 131072 | bytes 786432 | tf_op jit(solution)/shard_map/psum | solution.py:107
  279.1 154.9 %all-reduce.3 = bf16[2,1024,128]{2,1,0:T(8,128)(2,1)} all-reduce(f32[2,1024,128]{2,1,0:T(8,128)} %pad_maximum_fusion.2), channel_id=1, replica_groups=mesh['gx'=16,'gy'=32] {'gy'}, use_global_device_ids=true, to_apply=%region_1.0 | all-reduce | flops 262144 | bytes 1572864 | tf_op jit(solution)/shard_map/psum | solution.py:103
  434.0 1.4 fusion.10
  436.6 1.6 multiply_reduce_fusion
  (74 shorter events, 23.4 us)
Async XLA Ops:
  0.6 8.6 %copy-start.9 = (bf16[2,2,128,2,128]{4,3,2,1,0:T(2,128)(2,1)S(1)}, bf16[2,2,128,2,128]{4,3,2,1,0:T(2,128)(2,1)}, u32[]{:S(2)}) copy-start(bf16[2,2,128,2,128]{4,3,2,1,0:T(2,128)(2,1)} %param.8) | copy-start | bytes 786436
  2.4 122.0 %collective-permute-start = (bf16[1,2,128,2,128]{4,2,1,0,3:T(8,128)(2,1)}, bf16[1,2,128,2,128]{4,2,1,0,3:T(8,128)(2,1)S(1)}, u32[]{:S(2)}, u32[]{:S(2)}) collective-permute-start(bf16[1,2,128,2,128]{4,2,1,0,3:T(8,128)(2,1)} %get-tuple-element.24), channel_id=1, source_target_pairs={{0,32},{32,64},{64,96},{96,128},{128,160},{160,192},{192,224},{224... | collective-permute-start | bytes 393224 | tf_op jit(solution)/shard_map/ppermute | solution.py:15
  4.3 120.8 %collective-permute-start.1 = (bf16[1,2,128,2,128]{4,2,1,0,3:T(8,128)(2,1)}, bf16[1,2,128,2,128]{4,2,1,0,3:T(8,128)(2,1)}, u32[]{:S(2)}, u32[]{:S(2)}) collective-permute-start(bf16[1,2,128,2,128]{4,2,1,0,3:T(8,128)(2,1)} %get-tuple-element.23), channel_id=1, source_target_pairs={{32,0},{64,32},{96,64},{128,96},{160,128},{192,160},{224,192},{256... | collective-permute-start | bytes 393224 | tf_op jit(solution)/shard_map/ppermute | solution.py:16
  9.3 2.6 copy-start.10
  9.3 87.3 %copy-start.1 = (bf16[2,1024,512]{2,1,0:T(8,128)(2,1)S(1)}, bf16[2,1024,512]{2,1,0:T(8,128)(2,1)}, u32[]{:S(2)}) copy-start(bf16[2,1024,512]{2,1,0:T(8,128)(2,1)} %param.12) | copy-start | bytes 6291460
  12.1 87.0 %copy-start.4 = (bf16[2,2,128,2,128]{4,3,2,1,0:T(2,128)(2,1)S(1)}, bf16[2,2,128,2,128]{4,3,2,1,0:T(2,128)(2,1)}, u32[]{:S(2)}) copy-start(bf16[2,2,128,2,128]{4,3,2,1,0:T(2,128)(2,1)} %param.7) | copy-start | bytes 786436
  96.6 19.5 %copy-start.8 = (bf16[2,1024,128]{2,1,0:T(8,128)(2,1)}, bf16[2,1024,128]{2,1,0:T(8,128)(2,1)S(1)}, u32[]{:S(2)}) copy-start(bf16[2,1024,128]{2,1,0:T(8,128)(2,1)S(1)} %all_gather.7) | copy-start | bytes 1572868
  99.1 19.5 %copy-start.12 = (s32[2,2,4]{2,1,0:T(2,128)S(1)}, s32[2,2,4]{2,1,0:T(2,128)}, u32[]{:S(2)}) copy-start(s32[2,2,4]{2,1,0:T(2,128)} %param.11) | copy-start | bytes 196
  118.7 2.2 copy-start.2
  118.7 3.8 copy-start.7
  120.9 2.1 copy-start.6
  122.6 1.2 copy-start
  124.1 1.0 copy-start.5
  126.1 7.6 %collective-permute-start.2 = (bf16[4,1,128,2,128]{4,2,1,0,3:T(8,128)(2,1)S(1)}, bf16[4,1,128,2,128]{4,2,1,0,3:T(8,128)(2,1)S(1)}, u32[]{:S(2)}, u32[]{:S(2)}) collective-permute-start(bf16[4,1,128,2,128]{4,2,1,0,3:T(8,128)(2,1)S(1)} %get-tuple-element.19), channel_id=1, source_target_pairs={{0,1},{1,2},{2,3},{3,4},{4,5},{5,6},{6,7},{7,8},{8,9},{9,10},{10,1... | collective-permute-start | bytes 786440 | tf_op jit(solution)/shard_map/ppermute | solution.py:15
  127.4 10.4 %collective-permute-start.3 = (bf16[4,1,128,2,128]{4,2,1,0,3:T(8,128)(2,1)S(1)}, bf16[4,1,128,2,128]{4,2,1,0,3:T(8,128)(2,1)S(1)}, u32[]{:S(2)}, u32[]{:S(2)}) collective-permute-start(bf16[4,1,128,2,128]{4,2,1,0,3:T(8,128)(2,1)S(1)} %get-tuple-element.20), channel_id=1, source_target_pairs={{1,0},{2,1},{3,2},{4,3},{5,4},{6,5},{7,6},{8,7},{9,8},{10,9},{11,1... | collective-permute-start | bytes 786440 | tf_op jit(solution)/shard_map/ppermute | solution.py:16
  142.9 25.8 %collective-permute-start.4 = (f32[1,2,4,128,2,128]{5,3,1,0,4,2:T(8,128)}, f32[1,2,4,128,2,128]{5,3,1,0,4,2:T(8,128)}, u32[]{:S(2)}, u32[]{:S(2)}) collective-permute-start(f32[1,2,4,128,2,128]{5,3,1,0,4,2:T(8,128)} %get-tuple-element.12), channel_id=1, source_target_pairs={{32,0},{64,32},{96,64},{128,96},{160,128},{192,160},{224,192},{256... | collective-permute-start | bytes 3145736 | tf_op jit(solution)/shard_map/ppermute | solution.py:16
  144.8 23.8 %collective-permute-start.5 = (f32[1,2,4,128,2,128]{5,3,1,0,4,2:T(8,128)}, f32[1,2,4,128,2,128]{5,3,1,0,4,2:T(8,128)}, u32[]{:S(2)}, u32[]{:S(2)}) collective-permute-start(f32[1,2,4,128,2,128]{5,3,1,0,4,2:T(8,128)} %get-tuple-element.11), channel_id=1, source_target_pairs={{0,32},{32,64},{64,96},{96,128},{128,160},{160,192},{192,224},{224... | collective-permute-start | bytes 3145736 | tf_op jit(solution)/shard_map/ppermute | solution.py:15
  173.2 260.8 %copy-start.11 = (bf16[32,2,2,128]{3,2,1,0:T(2,128)(2,1)S(1)}, bf16[32,2,2,128]{3,2,1,0:T(2,128)(2,1)}, u32[]{:S(2)}) copy-start(bf16[32,2,2,128]{3,2,1,0:T(2,128)(2,1)} %param.13) | copy-start | bytes 98308
  173.2 263.4 %collective-permute-start.6 = (f32[4,1,4,128,2,128]{5,3,1,0,4,2:T(8,128)}, f32[4,1,4,128,2,128]{5,3,1,0,4,2:T(8,128)}, u32[]{:S(2)}, u32[]{:S(2)}) collective-permute-start(f32[4,1,4,128,2,128]{5,3,1,0,4,2:T(8,128)} %get-tuple-element.9), channel_id=1, source_target_pairs={{1,0},{2,1},{3,2},{4,3},{5,4},{6,5},{7,6},{8,7},{9,8},{10,9},{11,1... | collective-permute-start | bytes 6291464 | tf_op jit(solution)/shard_map/ppermute | solution.py:16
  174.6 262.0 %collective-permute-start.7 = (f32[4,1,4,128,2,128]{5,3,1,0,4,2:T(8,128)}, f32[4,1,4,128,2,128]{5,3,1,0,4,2:T(8,128)}, u32[]{:S(2)}, u32[]{:S(2)}) collective-permute-start(f32[4,1,4,128,2,128]{5,3,1,0,4,2:T(8,128)} %get-tuple-element.10), channel_id=1, source_target_pairs={{0,1},{1,2},{2,3},{3,4},{4,5},{5,6},{6,7},{7,8},{8,9},{9,10},{10,1... | collective-permute-start | bytes 6291464 | tf_op jit(solution)/shard_map/ppermute | solution.py:15
  434.0 2.7 copy-start.3
where the time goes:
time: 441 us; the launch traced here: 440 us
  blocking collectives  354 us (80%)
  waiting for transfers between devices  25.1 us (6%)
  starting transfers between devices  20.7 us (5%)
  matrix products  19 us (4%)
  local copies, waits for them, and re-layouts  12.8 us (3%)
  other arithmetic  6.95 us (2%)
    psum x1, blocking collectives, on_device(): pressure_band = lax.psum(pressure_part, 'gy')  155 us
    psum x1, blocking collectives, on_device(): reaction_band = lax.psum(reaction_part, 'gx')  98.1 us
    all_gather x1, blocking collectives, on_device(): piece = lax.all_gather(load_panels, 'gy', axis=1, tiled=True)  84.5 us
    ppermute x4, waiting for transfers between devices, extended(): after = lax.ppermute(first, axis, down)  22.1 us
    all_gather x1, blocking collectives, on_device(): piece = lax.all_gather(motion_panels, 'gx', axis=1, tiled=True)  16.8 us
    ppermute x4, starting transfers between devices, extended(): before = lax.ppermute(last, axis, up)  12.5 us
  transfers between devices with their start and end apart: 8, of which 3 were waited for; matrix products, arithmetic and copies ran while one was open for 5% of the time, Pallas kernels for 0%

commit v1 on v0

--- a/solution.py
+++ b/solution.py
@@ -96,7 +96,10 @@
     first = plain_product(hydro[0], piece[0]) - plain_product(hydro[1], piece[1])
     second = plain_product(hydro[0], piece[1]) + plain_product(hydro[1], piece[0])
     pressure_part = jnp.stack([first, second])
-    piece = lax.all_gather(load_panels, "gy", axis=1, tiled=True)
+    load_the_heaps = lambda m: jnp.concatenate(
+        lax.all_to_all(jnp.stack(lax.axis_size("gy") * [m]), "gy", split_axis=0, concat_axis=0), 1
+    )
+    piece = load_the_heaps(load_panels)
     first = flipped_product(hydro[0], piece[0]) + flipped_product(hydro[1], piece[1])
     second = flipped_product(hydro[0], piece[1]) - flipped_product(hydro[1], piece[0])
     reaction_part = jnp.stack([first, second])

time: 441 us -> 338 us (0.77)
  the two profiles are of different devices: /device:TPU:14 before, /device:TPU:1 now
where the time goes in v1:
time: 338 us
  blocking collectives  251 us (74%)
  starting transfers between devices  41 us (12%)
  matrix products  17.2 us (5%)
  local copies, waits for them, and re-layouts  14.3 us (4%)
  other arithmetic  7.74 us (2%)
  waiting for transfers between devices  5.52 us (2%)
    psum x1, blocking collectives, on_device(): pressure_band = lax.psum(pressure_part, 'gy')  132 us
    psum x1, blocking collectives, on_device(): reaction_band = lax.psum(reaction_part, 'gx')  97.7 us
    all_gather x1, blocking collectives, on_device(): piece = lax.all_gather(motion_panels, 'gx', axis=1, tiled=True)  20.6 us
    ppermute x4, starting transfers between devices, extended(): before = lax.ppermute(last, axis, up)  15.6 us
    all_to_all x1, starting transfers between devices, on_device(): lax.all_to_all(jnp.stack(lax.axis_size('gy') * [m]), 'gy', split_axis=0,...  14.1 us
    ppermute x4, starting transfers between devices, extended(): after = lax.ppermute(first, axis, down)  11.3 us
    dot_general x16, matrix products, mult(): return jnp.einsum(form, matrix, values, preferred_element_type=jnp.float32)  7.89 us
  transfers between devices with their start and end apart: 9, of which 2 were waited for; matrix products, arithmetic and copies ran while one was open for 10% of the time, Pallas kernels for 0%

profile of v1, /device:TPU:1, one launch (start us, length us, event | category | flops | bytes accessed | tf_op | source)
XLA Modules:
  0.0 337.7 jit_solution(4934027351917285798)
XLA Ops:
  2.5 4.6 %collective-permute-start = (bf16[1,2,128,2,128]{4,2,1,0,3:T(8,128)(2,1)}, bf16[1,2,128,2,128]{4,2,1,0,3:T(8,128)(2,1)S(1)}, u32[]{:S(2)}, u32[]{:S(2)}) collective-permute-start(bf16[1,2,128,2,128]{4,2,1,0,3:T(8,128)(2,1)} %get-tuple-element.26), channel_id=1, source_target_pairs={{0,32},{32,64},{64,96},{96,128},{128,160},{160,192},{192,224},{224... | collective-permute-start | bytes 393224 | tf_op jit(solution)/shard_map/ppermute | solution.py:15
  7.1 5.5 %collective-permute-start.1 = (bf16[1,2,128,2,128]{4,2,1,0,3:T(8,128)(2,1)}, bf16[1,2,128,2,128]{4,2,1,0,3:T(8,128)(2,1)}, u32[]{:S(2)}, u32[]{:S(2)}) collective-permute-start(bf16[1,2,128,2,128]{4,2,1,0,3:T(8,128)(2,1)} %get-tuple-element.25), channel_id=1, source_target_pairs={{32,0},{64,32},{96,64},{128,96},{160,128},{192,160},{224,192},{256... | collective-permute-start | bytes 393224 | tf_op jit(solution)/shard_map/ppermute | solution.py:16
  14.6 14.1 %all-to-all-start = ((bf16[32,2,32,128]{3,2,1,0:T(8,128)(2,1)}), bf16[32,2,32,128]{3,2,1,0:T(8,128)(2,1)}, u32[]{:S(2)}, u32[]{:S(2)}) async-start(bf16[32,2,32,128]{3,2,1,0:T(8,128)(2,1)} %stack.124), calls=%async_computation | async-start | bytes 1048576 | tf_op jit(solution)/shard_map/all_to_all | solution.py:100
  31.2 20.6 %all_gather.3 = bf16[2,512,128]{2,1,0:T(8,128)(2,1)S(1)} all-gather(bf16[2,32,128]{2,1,0:T(8,128)(2,1)S(1)} %fusion.20), channel_id=1, replica_groups=mesh['gx'=16,'gy'=32] {'gx'}, dimensions={1}, use_global_device_ids=true | all-gather | bytes 278528 | tf_op jit(solution)/shard_map/all_gather | solution.py:95
  52.7 1.3 fusion.2
  53.9 1.3 fusion.1
  59.2 3.4 collective-permute-start.2
  62.5 1.3 collective-permute-start.3
  66.0 2.4 collective-permute-done.2
  69.1 3.1 collective-permute-done.3
  76.5 1.3 maximum_multiply_fusion.1
  77.7 1.4 fusion.104
  79.2 3.2 collective-permute-start.4
  82.4 2.4 collective-permute-start.5
  84.7 132.5 %all-reduce.3 = bf16[2,1024,128]{2,1,0:T(8,128)(2,1)} all-reduce(f32[2,1024,128]{2,1,0:T(8,128)} %pad_maximum_fusion.2), channel_id=1, replica_groups=mesh['gx'=16,'gy'=32] {'gy'}, use_global_device_ids=true, to_apply=%region_1.0 | all-reduce | flops 262144 | bytes 1572864 | tf_op jit(solution)/shard_map/psum | solution.py:106
  217.3 1.9 pad_maximum_fusion
  219.2 2.5 fusion.103
  221.7 1.3 collective-permute-start.6
  223.0 5.3 %collective-permute-start.7 = (f32[4,1,4,128,2,128]{5,3,1,0,4,2:T(8,128)}, f32[4,1,4,128,2,128]{5,3,1,0,4,2:T(8,128)}, u32[]{:S(2)}, u32[]{:S(2)}) collective-permute-start(f32[4,1,4,128,2,128]{5,3,1,0,4,2:T(8,128)} %get-tuple-element.10), channel_id=1, source_target_pairs={{0,1},{1,2},{2,3},{3,4},{4,5},{5,6},{6,7},{7,8},{8,9},{9,10},{10,1... | collective-permute-start | bytes 6291464 | tf_op jit(solution)/shard_map/ppermute | solution.py:15
  228.5 1.4 fusion.10
  231.1 1.2 fusion.105
  232.4 1.8 fusion.25
  236.6 97.7 %all-reduce.2 = bf16[2,512,128]{2,1,0:T(8,128)(2,1)S(1)} all-reduce(f32[2,512,128]{2,1,0:T(8,128)} %pad_maximum_fusion.12), channel_id=1, replica_groups=mesh['gx'=16,'gy'=32] {'gx'}, use_global_device_ids=true, to_apply=%region_2.0 | all-reduce | flops 131072 | bytes 786432 | tf_op jit(solution)/shard_map/psum | solution.py:110
  334.3 1.6 multiply_reduce_fusion
  (77 shorter events, 23.7 us)
Async XLA Ops:
  0.6 28.1 %copy-start.8 = (bf16[2,2,128,2,128]{4,3,2,1,0:T(2,128)(2,1)S(1)}, bf16[2,2,128,2,128]{4,3,2,1,0:T(2,128)(2,1)}, u32[]{:S(2)}) copy-start(bf16[2,2,128,2,128]{4,3,2,1,0:T(2,128)(2,1)} %param.8) | copy-start | bytes 786436
  0.6 28.2 %copy-start.4 = (bf16[2,2,5,2,128,128]{5,4,3,2,1,0:T(8,128)(2,1)S(1)}, bf16[2,2,5,2,128,128]{5,4,3,2,1,0:T(8,128)(2,1)}, u32[]{:S(2)}) copy-start(bf16[2,2,5,2,128,128]{5,4,3,2,1,0:T(8,128)(2,1)} %param.10) | copy-start | bytes 3932164
  2.5 54.8 %collective-permute-start = (bf16[1,2,128,2,128]{4,2,1,0,3:T(8,128)(2,1)}, bf16[1,2,128,2,128]{4,2,1,0,3:T(8,128)(2,1)S(1)}, u32[]{:S(2)}, u32[]{:S(2)}) collective-permute-start(bf16[1,2,128,2,128]{4,2,1,0,3:T(8,128)(2,1)} %get-tuple-element.26), channel_id=1, source_target_pairs={{0,32},{32,64},{64,96},{96,128},{128,160},{160,192},{192,224},{224... | collective-permute-start | bytes 393224 | tf_op jit(solution)/shard_map/ppermute | solution.py:15
  7.1 50.4 %collective-permute-start.1 = (bf16[1,2,128,2,128]{4,2,1,0,3:T(8,128)(2,1)}, bf16[1,2,128,2,128]{4,2,1,0,3:T(8,128)(2,1)}, u32[]{:S(2)}, u32[]{:S(2)}) collective-permute-start(bf16[1,2,128,2,128]{4,2,1,0,3:T(8,128)(2,1)} %get-tuple-element.25), channel_id=1, source_target_pairs={{32,0},{64,32},{96,64},{128,96},{160,128},{192,160},{224,192},{256... | collective-permute-start | bytes 393224 | tf_op jit(solution)/shard_map/ppermute | solution.py:16
  14.6 216.5 %all-to-all-start = ((bf16[32,2,32,128]{3,2,1,0:T(8,128)(2,1)}), bf16[32,2,32,128]{3,2,1,0:T(8,128)(2,1)}, u32[]{:S(2)}, u32[]{:S(2)}) async-start(bf16[32,2,32,128]{3,2,1,0:T(8,128)(2,1)} %stack.124), calls=%async_computation | async-start | bytes 1048576 | tf_op jit(solution)/shard_map/all_to_all | solution.py:100
  29.2 1.8 copy-start.7
  29.2 1.8 copy-start.10
  29.2 22.6 %copy-start = (bf16[2,1024,512]{2,1,0:T(8,128)(2,1)S(1)}, bf16[2,1024,512]{2,1,0:T(8,128)(2,1)}, u32[]{:S(2)}) copy-start(bf16[2,1024,512]{2,1,0:T(8,128)(2,1)} %param.12) | copy-start | bytes 6291460
  57.1 7.6 %copy-start.12 = (s32[2,2,4]{2,1,0:T(2,128)S(1)}, s32[2,2,4]{2,1,0:T(2,128)}, u32[]{:S(2)}) copy-start(s32[2,2,4]{2,1,0:T(2,128)} %param.11) | copy-start | bytes 196
  59.2 9.2 %collective-permute-start.2 = (bf16[4,1,128,2,128]{4,2,1,0,3:T(8,128)(2,1)}, bf16[4,1,128,2,128]{4,2,1,0,3:T(8,128)(2,1)S(1)}, u32[]{:S(2)}, u32[]{:S(2)}) collective-permute-start(bf16[4,1,128,2,128]{4,2,1,0,3:T(8,128)(2,1)} %get-tuple-element.21), channel_id=1, source_target_pairs={{0,1},{1,2},{2,3},{3,4},{4,5},{5,6},{6,7},{7,8},{8,9},{9,10},{10,1... | collective-permute-start | bytes 786440 | tf_op jit(solution)/shard_map/ppermute | solution.py:15
  62.5 9.7 %collective-permute-start.3 = (bf16[4,1,128,2,128]{4,2,1,0,3:T(8,128)(2,1)}, bf16[4,1,128,2,128]{4,2,1,0,3:T(8,128)(2,1)}, u32[]{:S(2)}, u32[]{:S(2)}) collective-permute-start(bf16[4,1,128,2,128]{4,2,1,0,3:T(8,128)(2,1)} %get-tuple-element.22), channel_id=1, source_target_pairs={{1,0},{2,1},{3,2},{4,3},{5,4},{6,5},{7,6},{8,7},{9,8},{10,9},{11,1... | collective-permute-start | bytes 786440 | tf_op jit(solution)/shard_map/ppermute | solution.py:16
  68.4 0.7 copy-start.9
  74.9 1.2 copy-start.2
  74.9 1.5 copy-start.3
  79.2 138.1 %collective-permute-start.4 = (f32[1,2,4,128,2,128]{5,3,1,0,4,2:T(8,128)}, f32[1,2,4,128,2,128]{5,3,1,0,4,2:T(8,128)}, u32[]{:S(2)}, u32[]{:S(2)}) collective-permute-start(f32[1,2,4,128,2,128]{5,3,1,0,4,2:T(8,128)} %get-tuple-element.12), channel_id=1, source_target_pairs={{32,0},{64,32},{96,64},{128,96},{160,128},{192,160},{224,192},{256... | collective-permute-start | bytes 3145736 | tf_op jit(solution)/shard_map/ppermute | solution.py:16
  82.4 134.9 %collective-permute-start.5 = (f32[1,2,4,128,2,128]{5,3,1,0,4,2:T(8,128)}, f32[1,2,4,128,2,128]{5,3,1,0,4,2:T(8,128)}, u32[]{:S(2)}, u32[]{:S(2)}) collective-permute-start(f32[1,2,4,128,2,128]{5,3,1,0,4,2:T(8,128)} %get-tuple-element.11), channel_id=1, source_target_pairs={{0,32},{32,64},{64,96},{96,128},{128,160},{160,192},{192,224},{224... | collective-permute-start | bytes 3145736 | tf_op jit(solution)/shard_map/ppermute | solution.py:15
  219.2 9.1 %copy-start.6 = (f32[2,2,128,128]{3,2,1,0:T(8,128)S(1)}, f32[2,2,128,128]{3,2,1,0:T(8,128)}, u32[]{:S(2)}) copy-start(f32[2,2,128,128]{3,2,1,0:T(8,128)} %fusion.77) | copy-start | bytes 786436
  219.2 9.4 %copy-start.11 = (bf16[32,2,2,128]{3,2,1,0:T(2,128)(2,1)S(1)}, bf16[32,2,2,128]{3,2,1,0:T(2,128)(2,1)}, u32[]{:S(2)}) copy-start(bf16[32,2,2,128]{3,2,1,0:T(2,128)(2,1)} %param.13) | copy-start | bytes 98308
  221.7 112.6 %collective-permute-start.6 = (f32[4,1,4,128,2,128]{5,3,1,0,4,2:T(8,128)}, f32[4,1,4,128,2,128]{5,3,1,0,4,2:T(8,128)}, u32[]{:S(2)}, u32[]{:S(2)}) collective-permute-start(f32[4,1,4,128,2,128]{5,3,1,0,4,2:T(8,128)} %get-tuple-element.9), channel_id=1, source_target_pairs={{1,0},{2,1},{3,2},{4,3},{5,4},{6,5},{7,6},{8,7},{9,8},{10,9},{11,1... | collective-permute-start | bytes 6291464 | tf_op jit(solution)/shard_map/ppermute | solution.py:16
  223.0 111.3 %collective-permute-start.7 = (f32[4,1,4,128,2,128]{5,3,1,0,4,2:T(8,128)}, f32[4,1,4,128,2,128]{5,3,1,0,4,2:T(8,128)}, u32[]{:S(2)}, u32[]{:S(2)}) collective-permute-start(f32[4,1,4,128,2,128]{5,3,1,0,4,2:T(8,128)} %get-tuple-element.10), channel_id=1, source_target_pairs={{0,1},{1,2},{2,3},{3,4},{4,5},{5,6},{6,7},{7,8},{8,9},{9,10},{10,1... | collective-permute-start | bytes 6291464 | tf_op jit(solution)/shard_map/ppermute | solution.py:15
  231.1 3.0 copy-start.1
  235.2 99.1 %copy-start.5 = (f32[2,2,128,1,128]{4,2,1,0,3:T(8,128)S(1)}, f32[2,2,128,1,128]{4,2,1,0,3:T(8,128)}, u32[]{:S(2)}) copy-start(f32[2,2,128,1,128]{4,2,1,0,3:T(8,128)} %fusion.12) | copy-start | bytes 786436
